TPU v7x, 32 devices: a whole 2x2x4 slice. The times are simulated.
32 devices in a mesh: dp: 4 (over z), mp: 8 (over y, x, core).
Axes of the slice: x: 2, y: 2, z: 4, core: 2. Of those that a mesh axis runs over, the one named last changes fastest.
Arguments:
- behaviors: bfloat16 [32, 2048, 1024], P('dp', 'mp'), may hold values from -8 to 8
- candidates: bfloat16 [32, 2048, 128], P('dp', 'mp'), may hold values from -12 to 12
- lengths: int32 [32], P('dp'), may hold values from 128 to 1024
- bilinear: bfloat16 [2048, 2048], P('mp'), may hold values from -1 to 2
- norm_gain: float32 [2048], replicated, may hold values from 0.1 to 1.9
- w_gate: bfloat16 [2048, 8192], P('dp', 'mp'), may hold values from -0.125 to 0.125
- w_up: bfloat16 [2048, 8192], P('dp', 'mp'), may hold values from -0.125 to 0.125
- w_down: bfloat16 [8192, 2048], P('mp', 'dp'), may hold values from -0.0625 to 0.0625
Outputs:
- interest: bfloat16 [32, 2048, 128], P('dp', 'mp')
All inputs are finite; a program needn't handle non-finite values.
Results may differ from a plain program's by a relative error of at most 0.015.
Values may be sent and summed in bfloat16 or wider, within the bound.
No kernel may reach another device: no remote copies, remote signals or barrier semaphores. Data moves between devices by JAX's collectives and lax.ppermute only.
A program may use at most 64 MiB of HBM per device.

v0:
```python
import math
import jax
import jax.numpy as jnp
from jax import lax
from jax.sharding import PartitionSpec as P


def attention_weights(scores, live):
    masked = jnp.where(live, scores, -1e30)
    highest = jnp.max(masked, axis=-1, keepdims=True)
    expons = jnp.where(live, jnp.exp(masked - highest), 0.0)
    return (expons / jnp.sum(expons, axis=-1, keepdims=True)).astype(jnp.bfloat16)


def shards(behaviors, candidates, lengths, bilinear, norm_gain, w_gate, w_up, w_down):
    user_count, width_part, cand_count = candidates.shape
    feature_width = bilinear.shape[1]
    behavior_count = behaviors.shape[2]
    query_part = jnp.einsum(
        "ek,ukc->uec",
        bilinear,
        lax.all_gather(candidates, "mp", axis=1, tiled=True),
        preferred_element_type=jnp.float32,
    )
    query = query_part.astype(jnp.bfloat16)
    partial_value = jnp.einsum("ukc,ukl->ucl", query, behaviors, preferred_element_type=jnp.float32)
    scale = 1.0 / math.sqrt(feature_width)
    live = (
        lax.broadcasted_iota(jnp.int32, (user_count, 1, behavior_count), 2) < lengths[:, None, None]
    )
    share = lax.psum_scatter(partial_value, "mp", scatter_dimension=1, tiled=True)
    probs_share = attention_weights(share * scale, live)
    probs = lax.all_gather(probs_share, "mp", axis=1, tiled=True)
    pooled = jnp.einsum(
        "ucl,ukl->ukc", probs, behaviors, preferred_element_type=jnp.float32
    ).astype(jnp.bfloat16)
    whole = lax.all_gather(pooled, "mp", axis=1, tiled=True)
    values = whole.astype(jnp.float32)
    square_mean = jnp.mean(values * values, axis=1, keepdims=True)
    normed = (values * lax.rsqrt(square_mean + 1e-06) * norm_gain[None, :, None]).astype(
        jnp.bfloat16
    )
    gate = jnp.einsum(
        "ukc,kf->ucf",
        normed,
        lax.all_gather(w_gate, "dp", axis=0, tiled=True),
        preferred_element_type=jnp.float32,
    )
    upward = jnp.einsum(
        "ukc,kf->ucf",
        normed,
        lax.all_gather(w_up, "dp", axis=0, tiled=True),
        preferred_element_type=jnp.float32,
    )
    hidden = (jax.nn.silu(gate) * upward).astype(jnp.bfloat16)
    down_full = lax.all_gather(w_down, "dp", axis=1, tiled=True)
    result = lax.psum_scatter(
        jnp.einsum("ucf,fk->kuc", hidden, down_full, preferred_element_type=jnp.float32).astype(
            jnp.bfloat16
        ),
        "mp",
        scatter_dimension=0,
        tiled=True,
    ).astype(jnp.float32)
    return jnp.transpose(result, (1, 0, 2)).astype(jnp.bfloat16)


def solution(mesh):
    return jax.shard_map(
        shards,
        mesh=mesh,
        in_specs=(
            P("dp", "mp", None),
            P("dp", "mp", None),
            P("dp"),
            P("mp", None),
            P(),
            P("dp", "mp"),
            P("dp", "mp"),
            P("mp", "dp"),
        ),
        out_specs=P("dp", "mp", None),
        check_vma=False,
    )
```

profile of v0, /device:TPU:0, one launch (start us, length us, event | category | flops | bytes accessed | tf_op | source)
XLA Modules:
  0.0 498.7 jit_solution(1023455317639719504)
XLA Ops:
  6.5 0.7 all-gather.7.cloned.1.call-update
  7.3 0.0 reduce-scatter.3.cloned.1.call-start
  7.3 41.3 %all-gather.7.cloned.1.call-done = bf16[8,2048,128]{2,1,0:T(8,128)(2,1)} async-done(((bf16[8,256,128]{2,1,0:T(8,128)(2,1)}), bf16[8,2048,128]{2,1,0:T(8,128)(2,1)}) %all-gather.7.cloned.1.call-update) | async-done | bytes 4194320 | tf_op jit(solution)/shard_map/all_gather | solution.py:22
  48.6 8.2 %fusion.24 = f32[8,128,1024]{2,1,0:T(8,128)} fusion(bf16[8,256,1024]{2,1,0:T(8,128)(2,1)} %param.8, bf16[8,2048,128]{2,1,0:T(8,128)(2,1)} %all-gather.7.cloned.1.call-done, bf16[256,2048]{1,0:T(8,128)(2,1)S(1)} %copy-done), kind=kOutput, calls=%fused_computation.18 | convolution fusion | flops 1610874880 | bytes 13631488 | tf_op jit(solution)/shard_map/ukc,ukl->ucl/dot_general | solution.py:26
  56.7 0.0 reduce-scatter.3.cloned.1.call-update
  56.8 0.0 all-gather.9.cloned.1.call-start
  56.8 0.6 copy-done.1
  57.4 0.1 iota_compare_fusion
  57.5 50.5 %reduce-scatter.3.cloned.1.call-done = f32[8,16,1024]{2,1,0:T(8,128)} async-done(((f32[8,128,1024]{2,1,0:T(8,128)}), f32[8,16,1024]{2,1,0:T(8,128)}) %reduce-scatter.3.cloned.1.call-update) | async-done | bytes 524304 | tf_op jit(solution)/shard_map/reduce_scatter | solution.py:31
  108.0 1.7 fusion.37
  109.7 0.8 divide_convert_fusion
  110.5 0.0 all-gather.9.cloned.1.call-update
  110.6 0.0 all-gather.11.cloned.1.call-start
  110.6 27.9 %all-gather.9.cloned.1.call-done = bf16[8,128,1024]{2,1,0:T(8,128)(2,1)} async-done(((bf16[8,16,1024]{2,1,0:T(8,128)(2,1)}), bf16[8,128,1024]{2,1,0:T(8,128)(2,1)}) %all-gather.9.cloned.1.call-update) | async-done | bytes 2097168 | tf_op jit(solution)/shard_map/all_gather | solution.py:33
  138.5 5.2 %fusion.27 = bf16[8,256,128]{1,2,0:T(8,128)(2,1)} fusion(bf16[8,128,1024]{2,1,0:T(8,128)(2,1)} %all-gather.9.cloned.1.call-done, bf16[8,256,1024]{2,1,0:T(8,128)(2,1)} %param.8), kind=kOutput, calls=%fused_computation.21 | convolution fusion | flops 537133056 | bytes 6815744 | tf_op jit(solution)/shard_map/ucl,ukl->ukc/dot_general | solution.py:34
  143.7 0.0 all-gather.13.cloned.1.call-start
  143.7 0.5 all-gather.13.cloned.1.call-update
  144.3 0.0 all-gather.15.cloned.1.call-start
  144.3 0.5 all-gather.15.cloned.1.call-update
  144.8 0.0 all-gather.17.cloned.1.call-start
  144.9 0.7 all-gather.17.cloned.1.call-update
  145.6 0.2 reduce-scatter.5.cloned.1.call-start
  145.8 35.4 %all-gather.11.cloned.1.call-done = bf16[8,2048,128]{1,2,0:T(8,128)(2,1)} async-done(((bf16[8,256,128]{1,2,0:T(8,128)(2,1)}), bf16[8,2048,128]{1,2,0:T(8,128)(2,1)}) %all-gather.11.cloned.1.call-update) | async-done | bytes 4194320 | tf_op jit(solution)/shard_map/all_gather | solution.py:37
  181.2 3.1 fusion.1
  184.3 79.1 %all-gather.13.cloned.1.call-done = bf16[2048,1024]{1,0:T(8,128)(2,1)} async-done(((bf16[512,1024]{1,0:T(8,128)(2,1)}), bf16[2048,1024]{1,0:T(8,128)(2,1)}) %all-gather.13.cloned.1.call-update) | async-done | bytes 4194320 | tf_op jit(solution)/shard_map/all_gather | solution.py:46
  263.4 9.9 %fusion.8 = f32[8,128,1024]{2,1,0:T(8,128)} fusion(bf16[2048,1024]{1,0:T(8,128)(2,1)} %all-gather.13.cloned.1.call-done, bf16[8,2048,128]{1,2,0:T(8,128)(2,1)} %all-gather.11.cloned.1.call-done, f32[2048]{0:T(1024)S(1)} %copy-done.2, f32[8,128]{1,0:T(8,128)S(1)} %add_rsqrt_fusion), kind=kOutput, calls=%fused_computation.10 | convolution fusion | flops 4303355904 | bytes 12595200 | tf_op jit(solution)/shard_map/ukc,kf->ucf/dot_general | solution.py:43
  273.3 70.7 %all-gather.15.cloned.1.call-done = bf16[2048,1024]{1,0:T(8,128)(2,1)} async-done(((bf16[512,1024]{1,0:T(8,128)(2,1)}), bf16[2048,1024]{1,0:T(8,128)(2,1)}) %all-gather.15.cloned.1.call-update) | async-done | bytes 4194320 | tf_op jit(solution)/shard_map/all_gather | solution.py:52
  344.0 80.8 %all-gather.17.cloned.1.call-done = bf16[1024,2048]{1,0:T(8,128)(2,1)} async-done(((bf16[1024,512]{1,0:T(8,128)(2,1)}), bf16[1024,2048]{1,0:T(8,128)(2,1)}) %all-gather.17.cloned.1.call-update) | async-done | bytes 4194320 | tf_op jit(solution)/shard_map/all_gather | solution.py:56
  424.9 15.2 %convert_bitcast_fusion = bf16[2048,8,128]{0,2,1:T(8,128)(2,1)} fusion(bf16[1024,2048]{1,0:T(8,128)(2,1)} %all-gather.17.cloned.1.call-done, f32[8,128,1024]{2,1,0:T(8,128)} %fusion.8, bf16[2048,1024]{1,0:T(8,128)(2,1)} %all-gather.15.cloned.1.call-done, bf16[8,2048,128]{1,2,0:T(8,128)(2,1)} %all-gather.11.cloned.1.call-done, f32[2048]{0:T(1024)S(1)} %copy-done.2, ...), kind=kOutput, calls=%fused_computation.12 | convolution fusion | flops 8606711808 | bytes 20983808 | tf_op jit(solution)/shard_map/ucf,fk->kuc/dot_general | solution.py:58
  440.1 0.0 reduce-scatter.5.cloned.1.call-update
  440.1 49.7 %reduce-scatter.5.cloned.1.call-done = bf16[256,8,128]{0,2,1:T(8,128)(2,1)} async-done(((bf16[2048,8,128]{0,2,1:T(8,128)(2,1)}), bf16[256,8,128]{0,2,1:T(8,128)(2,1)}) %reduce-scatter.5.cloned.1.call-update) | async-done | bytes 524304 | tf_op jit(solution)/shard_map/reduce_scatter | solution.py:57
  489.8 2.0 copy.9
  (8 shorter events, 0.0 us)
Async XLA Ops:
  6.5 42.0 %copy-start = (bf16[256,2048]{1,0:T(8,128)(2,1)S(1)}, bf16[256,2048]{1,0:T(8,128)(2,1)}, u32[]{:S(2)}) copy-start(bf16[256,2048]{1,0:T(8,128)(2,1)} %param.11) | copy-start | bytes 3145732
  6.5 42.0 %all-gather.7.cloned.1.call-start = ((), (), s32[]{:S(2)}) async-start(), calls=%async_computation.2 | async-start | bytes 4718592 | tf_op jit(solution)/shard_map/all_gather | solution.py:22
  7.3 100.8 %reduce-scatter.3.cloned.1.call-start = ((), (), s32[]{:S(2)}) async-start(), calls=%async_computation.3 | async-start | bytes 4718592 | tf_op jit(solution)/shard_map/reduce_scatter | solution.py:31
  56.7 0.7 copy-start.1
  56.8 81.7 %all-gather.9.cloned.1.call-start = ((), (), s32[]{:S(2)}) async-start(), calls=%async_computation.4 | async-start | bytes 2359296 | tf_op jit(solution)/shard_map/all_gather | solution.py:33
  110.6 70.6 %all-gather.11.cloned.1.call-start = ((), (), s32[]{:S(2)}) async-start(), calls=%async_computation.5 | async-start | bytes 4718592 | tf_op jit(solution)/shard_map/all_gather | solution.py:37
  143.7 119.7 %copy-start.2 = (f32[2048]{0:T(1024)S(1)}, f32[2048]{0:T(1024)}, u32[]{:S(2)}) copy-start(f32[2048]{0:T(1024)} %param.12) | copy-start | bytes 24580
  143.7 119.7 %all-gather.13.cloned.1.call-start = ((), (), s32[]{:S(2)}) async-start(), calls=%async_computation.6 | async-start | bytes 5242880 | tf_op jit(solution)/shard_map/all_gather | solution.py:46
  144.3 199.8 %all-gather.15.cloned.1.call-start = ((), (), s32[]{:S(2)}) async-start(), calls=%async_computation.7 | async-start | bytes 5242880 | tf_op jit(solution)/shard_map/all_gather | solution.py:52
  144.8 280.0 %all-gather.17.cloned.1.call-start = ((), (), s32[]{:S(2)}) async-start(), calls=%async_computation.8 | async-start | bytes 5242880 | tf_op jit(solution)/shard_map/all_gather | solution.py:56
  145.6 344.2 %reduce-scatter.5.cloned.1.call-start = ((), (), s32[]{:S(2)}) async-start(), calls=%async_computation.9 | async-start | bytes 4718592 | tf_op jit(solution)/shard_map/reduce_scatter | solution.py:57
Sparse Core Ops, SparseCore 0:
  9.2 39.2 all-gather.6
  56.9 51.0 reduce-scatter.2
  110.7 27.7 all-gather.8
  143.8 37.3 all-gather.10
  182.6 80.7 all-gather.12
  264.8 79.2 all-gather.14
  345.6 79.2 all-gather.16
  440.2 49.5 reduce-scatter.4
where the time goes:
time: 499 us
  waiting for transfers between devices  438 us (88%)
  matrix products  38.4 us (8%)
  between operations  13.5 us (3%)
  other arithmetic  5.68 us (1%)
    all_gather x1, waiting for transfers between devices, shards(): down_full = lax.all_gather(w_down, 'dp', axis=1, tiled=True)  80.8 us
    all_gather x1, waiting for transfers between devices, shards(): lax.all_gather(w_gate, 'dp', axis=0, tiled=True)  79.1 us
    all_gather x1, waiting for transfers between devices, shards(): lax.all_gather(w_up, 'dp', axis=0, tiled=True)  70.7 us
    reduce_scatter x1, waiting for transfers between devices, shards(): lax.psum_scatter(partial_value, 'mp', scatter_dimension=1, tiled=True)  50.5 us
    reduce_scatter x1, waiting for transfers between devices, shards(): lax.psum_scatter(jnp.einsum('ucf,fk->kuc', hidden, down_full, preferred_e...  49.7 us
    all_gather x1, waiting for transfers between devices, shards(): lax.all_gather(candidates, 'mp', axis=1, tiled=True)  41.3 us
    all_gather x1, waiting for transfers between devices, shards(): whole = lax.all_gather(pooled, 'mp', axis=1, tiled=True)  35.4 us
    all_gather x1, waiting for transfers between devices, shards(): probs = lax.all_gather(probs_share, 'mp', axis=1, tiled=True)  27.9 us
  transfers between devices with their start and end apart: 8, of which 8 were waited for; matrix products, arithmetic and copies ran while one was open for 3% of the time, Pallas kernels for 0%

commit v1 on v0

--- a/solution.py
+++ b/solution.py
@@ -53,7 +53,12 @@
         preferred_element_type=jnp.float32,
     )
     hidden = (jax.nn.silu(gate) * upward).astype(jnp.bfloat16)
-    down_full = lax.all_gather(w_down, "dp", axis=1, tiled=True)
+    ring = [w_down]
+    for hop in range(3):
+        ring.append(lax.ppermute(ring[-1], "dp", [(dev, (dev + 1) % 4) for dev in range(4)]))
+    down_full = jnp.roll(
+        jnp.concatenate(ring[::-1], axis=1), (lax.axis_index("dp") + 1) * ring[0].shape[1], axis=1
+    )
     result = lax.psum_scatter(
         jnp.einsum("ucf,fk->kuc", hidden, down_full, preferred_element_type=jnp.float32).astype(
             jnp.bfloat16

time: 499 us -> 442 us (0.89)
  waiting for transfers between devices: 438 us -> 367 us
  local copies, waits for them, and re-layouts: 2.63 us -> 14.5 us
    ppermute x0 -> x3, waiting for transfers between devices: none -> 106 us  [shards(): lax.ppermute(ring[-1], 'dp', [(dev, (dev + 1) % 4) for dev in range(4)])]
    all_gather x1 -> x0, waiting for transfers between devices: 80.8 us -> none  [shards(): down_full = lax.all_gather(w_down, 'dp', axis=1, tiled=True)]
    all_gather x1, waiting for transfers between devices: 70.7 us -> 20 us  [shards(): lax.all_gather(w_up, 'dp', axis=0, tiled=True)]
    all_gather x1, waiting for transfers between devices: 35.4 us -> 0.01 us  [shards(): whole = lax.all_gather(pooled, 'mp', axis=1, tiled=True)]
    unnamed x6 -> x16, local copies, waits for them, and re-layouts: 0.59 us -> 13.5 us
    all_gather x1, waiting for transfers between devices: 79.1 us -> 69.5 us  [shards(): lax.all_gather(w_gate, 'dp', axis=0, tiled=True)]
  transfers between devices with their start and end apart: 8 -> 10, of which waited for: 8 -> 9; matrix products, arithmetic and copies ran while one was open for 3% -> 6% of each run, Pallas kernels for 0% -> 0%
where the time goes in v1:
time: 442 us; the launch traced here: 441 us
  waiting for transfers between devices  367 us (83%)
  matrix products  39.1 us (9%)
  local copies, waits for them, and re-layouts  14.5 us (3%)
  between operations  13.5 us (3%)
  other arithmetic  5.65 us (1%)
    ppermute x3, waiting for transfers between devices, shards(): lax.ppermute(ring[-1], 'dp', [(dev, (dev + 1) % 4) for dev in range(4)])  106 us
    all_gather x1, waiting for transfers between devices, shards(): lax.all_gather(w_gate, 'dp', axis=0, tiled=True)  69.5 us
    reduce_scatter x1, waiting for transfers between devices, shards(): lax.psum_scatter(partial_value, 'mp', scatter_dimension=1, tiled=True)  50.5 us
    reduce_scatter x1, waiting for transfers between devices, shards(): lax.psum_scatter(jnp.einsum('ucf,fk->kuc', hidden, down_full, preferred_e...  49.7 us
    all_gather x1, waiting for transfers between devices, shards(): lax.all_gather(candidates, 'mp', axis=1, tiled=True)  41.3 us
    all_gather x1, waiting for transfers between devices, shards(): probs = lax.all_gather(probs_share, 'mp', axis=1, tiled=True)  27.9 us
    all_gather x1, waiting for transfers between devices, shards(): lax.all_gather(w_up, 'dp', axis=0, tiled=True)  20 us
    dot_general x1, matrix products, shards(): jnp.einsum('ucf,fk->kuc', hidden, down_full, preferred_element_type=jnp.f...  15.8 us
  transfers between devices with their start and end apart: 10, of which 9 were waited for; matrix products, arithmetic and copies ran while one was open for 6% of the time, Pallas kernels for 0%

profile of v1, /device:TPU:0, one launch (start us, length us, event | category | flops | bytes accessed | tf_op | source)
XLA Modules:
  0.0 441.2 jit_solution(1074521576066140140)
XLA Ops:
  6.5 0.7 all-gather.6.cloned.1.call-update
  7.3 41.3 %all-gather.6.cloned.1.call-done = bf16[8,2048,128]{2,1,0:T(8,128)(2,1)} async-done(((bf16[8,256,128]{2,1,0:T(8,128)(2,1)}), bf16[8,2048,128]{2,1,0:T(8,128)(2,1)}) %all-gather.6.cloned.1.call-update) | async-done | bytes 4194320 | tf_op jit(solution)/shard_map/all_gather | solution.py:22
  48.6 8.2 %fusion.18 = f32[8,128,1024]{2,1,0:T(8,128)} fusion(bf16[8,256,1024]{2,1,0:T(8,128)(2,1)} %param.8, bf16[8,2048,128]{2,1,0:T(8,128)(2,1)} %all-gather.6.cloned.1.call-done, bf16[256,2048]{1,0:T(8,128)(2,1)S(1)} %copy-done), kind=kOutput, calls=%fused_computation.19 | convolution fusion | flops 1610874880 | bytes 13631488 | tf_op jit(solution)/shard_map/ukc,ukl->ucl/dot_general | solution.py:26
  56.8 0.0 all-gather.8.cloned.1.call-start
  56.8 0.6 copy-done.2
  57.4 0.1 iota_compare_fusion
  57.5 50.5 %reduce-scatter.3.cloned.1.call-done = f32[8,16,1024]{2,1,0:T(8,128)} async-done(((f32[8,128,1024]{2,1,0:T(8,128)}), f32[8,16,1024]{2,1,0:T(8,128)}) %reduce-scatter.3.cloned.1.call-update) | async-done | bytes 524304 | tf_op jit(solution)/shard_map/reduce_scatter | solution.py:31
  108.0 1.6 fusion.40
  109.7 0.8 divide_convert_fusion
  110.6 27.9 %all-gather.8.cloned.1.call-done = bf16[8,128,1024]{2,1,0:T(8,128)(2,1)} async-done(((bf16[8,16,1024]{2,1,0:T(8,128)(2,1)}), bf16[8,128,1024]{2,1,0:T(8,128)(2,1)}) %all-gather.8.cloned.1.call-update) | async-done | bytes 2097168 | tf_op jit(solution)/shard_map/all_gather | solution.py:33
  138.4 5.1 %fusion.21 = bf16[8,256,128]{1,2,0:T(8,128)(2,1)} fusion(bf16[8,128,1024]{2,1,0:T(8,128)(2,1)} %all-gather.8.cloned.1.call-done, bf16[8,256,1024]{2,1,0:T(8,128)(2,1)} %param.8), kind=kOutput, calls=%fused_computation.22 | convolution fusion | flops 537133056 | bytes 6815744 | tf_op jit(solution)/shard_map/ucl,ukl->ukc/dot_general | solution.py:34
  143.7 0.5 all-gather.14.cloned.1.call-update
  144.3 0.5 all-gather.12.cloned.1.call-update
  144.8 0.5 copy.9
  145.4 1.5 collective-permute-start
  146.9 25.6 %collective-permute-done = bf16[1024,512]{0,1:T(8,128)(2,1)S(1)} collective-permute-done((bf16[1024,512]{0,1:T(8,128)(2,1)S(1)}, bf16[1024,512]{0,1:T(8,128)(2,1)S(1)}, u32[]{:S(2)}, u32[]{:S(2)}) %collective-permute-start) | collective-permute-done | bytes 1048608 | tf_op jit(solution)/shard_map/ppermute | solution.py:58
  172.5 31.4 %collective-permute-done.1 = bf16[1024,512]{0,1:T(8,128)(2,1)} collective-permute-done((bf16[1024,512]{0,1:T(8,128)(2,1)S(1)}, bf16[1024,512]{0,1:T(8,128)(2,1)}, u32[]{:S(2)}, u32[]{:S(2)}) %collective-permute-start.1) | collective-permute-done | bytes 1048608 | tf_op jit(solution)/shard_map/ppermute | solution.py:58
  203.9 48.8 %collective-permute-done.2 = bf16[1024,512]{0,1:T(8,128)(2,1)} collective-permute-done((bf16[1024,512]{0,1:T(8,128)(2,1)}, bf16[1024,512]{0,1:T(8,128)(2,1)}, u32[]{:S(2)}, u32[]{:S(2)}) %collective-permute-start.2) | collective-permute-done | bytes 1048608 | tf_op jit(solution)/shard_map/ppermute | solution.py:58
  252.7 2.3 constant_dynamic-update-slice_fusion.7
  255.0 2.3 constant_dynamic-update-slice_fusion.6
  257.3 1.0 constant_dynamic-update-slice_fusion.5
  258.3 1.1 constant_dynamic-update-slice_fusion.4
  259.4 2.3 constant_dynamic-update-slice_fusion.3
  261.6 2.3 constant_dynamic-update-slice_fusion.2
  263.9 1.1 constant_dynamic-update-slice_fusion.1
  265.0 1.1 constant_dynamic-update-slice_fusion
  266.1 3.1 fusion.1
  269.2 20.0 %all-gather.14.cloned.1.call-done = bf16[2048,1024]{1,0:T(8,128)(2,1)} async-done(((bf16[512,1024]{1,0:T(8,128)(2,1)}), bf16[2048,1024]{1,0:T(8,128)(2,1)}) %all-gather.14.cloned.1.call-update) | async-done | bytes 4194320 | tf_op jit(solution)/shard_map/all_gather | solution.py:52
  289.3 10.0 %fusion.4 = f32[8,128,1024]{2,1,0:T(8,128)} fusion(bf16[2048,1024]{1,0:T(8,128)(2,1)} %all-gather.14.cloned.1.call-done, bf16[8,2048,128]{1,2,0:T(8,128)(2,1)} %all-gather.10.cloned.1.call-done, f32[2048]{0:T(1024)S(1)} %copy-done.3, f32[8,128]{1,0:T(8,128)S(1)} %add_rsqrt_fusion), kind=kOutput, calls=%fused_computation.6 | convolution fusion | flops 4303355904 | bytes 12595200 | tf_op jit(solution)/shard_map/ukc,kf->ucf/dot_general | solution.py:49
  299.2 69.5 %all-gather.12.cloned.1.call-done = bf16[2048,1024]{1,0:T(8,128)(2,1)} async-done(((bf16[512,1024]{1,0:T(8,128)(2,1)}), bf16[2048,1024]{1,0:T(8,128)(2,1)}) %all-gather.12.cloned.1.call-update) | async-done | bytes 4194320 | tf_op jit(solution)/shard_map/all_gather | solution.py:46
  368.8 15.8 %fusion.11 = bf16[2048,8,128]{2,0,1:T(8,128)(2,1)} fusion(bf16[1024,4096]{0,1:T(8,128)(2,1)} %constant_dynamic-update-slice_fusion, s32[]{:T(128)S(6)} %select_n.21, f32[8,128,1024]{2,1,0:T(8,128)} %fusion.4, bf16[2048,1024]{1,0:T(8,128)(2,1)} %all-gather.12.cloned.1.call-done, bf16[8,2048,128]{1,2,0:T(8,128)(2,1)} %all-gather.10.cloned.1.call-done, ...), kind=kOutput, calls=%fused_computation.14 | convolution fusion | flops 8606711808 | bytes 20983812 | tf_op jit(solution)/shard_map/ucf,fk->kuc/dot_general | solution.py:63
  384.6 49.7 %reduce-scatter.5.cloned.1.call-done = bf16[256,8,128]{2,0,1:T(8,128)(2,1)} async-done(((bf16[2048,8,128]{2,0,1:T(8,128)(2,1)}), bf16[256,8,128]{2,0,1:T(8,128)(2,1)}) %reduce-scatter.5.cloned.1.call-update) | async-done | bytes 524304 | tf_op jit(solution)/shard_map/reduce_scatter | solution.py:62
  (21 shorter events, 0.3 us)
Async XLA Ops:
  6.5 42.0 %copy-start = (bf16[256,2048]{1,0:T(8,128)(2,1)S(1)}, bf16[256,2048]{1,0:T(8,128)(2,1)}, u32[]{:S(2)}) copy-start(bf16[256,2048]{1,0:T(8,128)(2,1)} %param.11) | copy-start | bytes 3145732
  6.5 42.0 %all-gather.6.cloned.1.call-start = ((), (), s32[]{:S(2)}) async-start(), calls=%async_computation.2 | async-start | bytes 4718592 | tf_op jit(solution)/shard_map/all_gather | solution.py:22
  7.3 100.8 %reduce-scatter.3.cloned.1.call-start = ((), (), s32[]{:S(2)}) async-start(), calls=%async_computation.3 | async-start | bytes 4718592 | tf_op jit(solution)/shard_map/reduce_scatter | solution.py:31
  56.7 0.7 copy-start.2
  56.8 81.7 %all-gather.8.cloned.1.call-start = ((), (), s32[]{:S(2)}) async-start(), calls=%async_computation.4 | async-start | bytes 2359296 | tf_op jit(solution)/shard_map/all_gather | solution.py:33
  110.5 34.3 %copy-start.1 = (bf16[1024,512]{1,0:T(8,128)(2,1)S(1)}, bf16[1024,512]{1,0:T(8,128)(2,1)}, u32[]{:S(2)}) copy-start(bf16[1024,512]{1,0:T(8,128)(2,1)} %param.15) | copy-start | bytes 3145732
  110.5 155.6 %all-gather.10.cloned.1.call-start = ((), (), s32[]{:S(2)}) async-start(), calls=%async_computation.5 | async-start | bytes 4718592 | tf_op jit(solution)/shard_map/all_gather | solution.py:37
  143.6 145.6 %all-gather.14.cloned.1.call-start = ((), (), s32[]{:S(2)}) async-start(), calls=%async_computation.7 | async-start | bytes 5242880 | tf_op jit(solution)/shard_map/all_gather | solution.py:52
  144.2 224.6 %all-gather.12.cloned.1.call-start = ((), (), s32[]{:S(2)}) async-start(), calls=%async_computation.6 | async-start | bytes 5242880 | tf_op jit(solution)/shard_map/all_gather | solution.py:46
  144.8 289.6 %reduce-scatter.5.cloned.1.call-start = ((), (), s32[]{:S(2)}) async-start(), calls=%async_computation.8 | async-start | bytes 4718592 | tf_op jit(solution)/shard_map/reduce_scatter | solution.py:62
  145.4 27.1 %collective-permute-start = (bf16[1024,512]{0,1:T(8,128)(2,1)S(1)}, bf16[1024,512]{0,1:T(8,128)(2,1)S(1)}, u32[]{:S(2)}, u32[]{:S(2)}) collective-permute-start(bf16[1024,512]{0,1:T(8,128)(2,1)S(1)} %copy.9), channel_id=1, source_target_pairs={{0,8},{8,16},{16,24},{24,0},{1,9},{9,17},{17,25},{25,1},{2,10},{10... | collective-permute-start | bytes 3145736 | tf_op jit(solution)/shard_map/ppermute | solution.py:58
  172.5 31.4 %collective-permute-start.1 = (bf16[1024,512]{0,1:T(8,128)(2,1)S(1)}, bf16[1024,512]{0,1:T(8,128)(2,1)}, u32[]{:S(2)}, u32[]{:S(2)}) collective-permute-start(bf16[1024,512]{0,1:T(8,128)(2,1)S(1)} %collective-permute-done), channel_id=1, source_target_pairs={{0,8},{8,16},{16,24},{24,0},{1,9},{9,17},{17,25},{25,1},{2,10},{10... | collective-permute-start | bytes 3145736 | tf_op jit(solution)/shard_map/ppermute | solution.py:58
  203.9 48.8 %collective-permute-start.2 = (bf16[1024,512]{0,1:T(8,128)(2,1)}, bf16[1024,512]{0,1:T(8,128)(2,1)}, u32[]{:S(2)}, u32[]{:S(2)}) collective-permute-start(bf16[1024,512]{0,1:T(8,128)(2,1)} %collective-permute-done.1), channel_id=1, source_target_pairs={{0,8},{8,16},{16,24},{24,0},{1,9},{9,17},{17,25},{25,1},{2,10},{10... | collective-permute-start | bytes 3145736 | tf_op jit(solution)/shard_map/ppermute | solution.py:58
  263.9 25.3 %copy-start.3 = (f32[2048]{0:T(1024)S(1)}, f32[2048]{0:T(1024)}, u32[]{:S(2)}) copy-start(f32[2048]{0:T(1024)} %param.12) | copy-start | bytes 24580
Sparse Core Ops, SparseCore 0:
  9.2 39.2 all-gather.5
  56.9 51.0 reduce-scatter.2
  110.6 27.7 all-gather.7
  143.7 37.3 all-gather.9
  182.5 106.6 all-gather.13
  290.7 78.0 all-gather.11
  384.7 49.5 reduce-scatter.4
